TPU v7x, 128 devices: a whole 4x4x4 slice. The times are simulated.
128 devices in a mesh: img: 16 (over z_lo, x, core), head: 2 (over z_hi), txt: 4 (over y).
Axes of the slice: x: 4, y: 4, z: 4 (z_hi: 2, z_lo: 2; z = z_hi * 2 + z_lo), core: 2. Of those that a mesh axis runs over, the one named last changes fastest.
Arguments:
- image_feats: bfloat16 [16384, 7680], P(('img', 'txt'), 'head'), may hold values from -6 to 6
- key_weight: bfloat16 [7680, 512], P('head'), may hold values from -0.0625 to 0.0625
- value_weight: bfloat16 [7680, 512], P('head'), may hold values from -0.0625 to 0.0625
- queries: bfloat16 [1024, 4096], P('txt', 'head'), may hold values from -21 to 21
- grad_out: bfloat16 [1024, 4096], P('txt', 'head'), may hold values from -768 to 768
- tile_image: int32 [128], P('img'), may hold values from 0 to 7, never falling along the last dimension, each value on 1 to 32 neighbouring positions
- text_sees: int32 [8, 8], replicated, may hold values from 0 to 1, as said below
Outputs:
- attn_out: bfloat16 [1024, 4096], P('txt', 'head')
- grad_feats: bfloat16 [16384, 7680], P(('img', 'txt'), 'head')
Inputs may be any that keep to these rules, and one draw needn't show every extreme that they name: `text_sees`: every row holds at least one 1.
All inputs are finite; a program needn't handle non-finite values.
Results may differ from a plain program's by a relative error of at most 0.012.
The roundings to bfloat16 on the way count: a program that leaves them out, or rounds other values in their place, can miss the bound.
Values may be sent and summed in bfloat16 or wider, within the bound.
No kernel may reach another device: no remote copies, remote signals or barrier semaphores. Data moves between devices by JAX's collectives and lax.ppermute only.
A program may use at most 128 MiB of HBM per device.

v0:
```python
import math
import jax
import jax.numpy as jnp
from jax import lax
from jax.sharding import PartitionSpec as P

HD = 128
TILE = 128
TBLK = 128


def in_blocks(array, dim, length):
    before, after = (array.shape[:dim], array.shape[dim + 1 :])
    return jnp.moveaxis(array.reshape(*before, length, -1, *after), dim, 0)


def summed_on_arrival(array, axis, dim):
    length = lax.axis_size(axis)
    blocks = lax.all_to_all(in_blocks(array, dim, length), axis, 0, 0, tiled=True)
    return jnp.sum(blocks, axis=0)


def in_one_piece(arrays, axis, dim, along):
    ends, at = ([], 0)
    for a in arrays[:-1]:
        at += a.shape[along]
        ends.append(at)
    both = jnp.concatenate(arrays, axis=along)
    return tuple(jnp.split(summed_on_arrival(both, axis, dim), ends, axis=along))


def sent_to_all(array, axis):
    copies = jnp.broadcast_to(array, (lax.axis_size(axis), *array.shape))
    return lax.all_to_all(copies, axis, split_axis=0, concat_axis=0, tiled=True)


def of_everyone(array, axis):
    everything = sent_to_all(array, axis)
    return jnp.max(everything, axis=0)


def of_everyone_2(array, axis):
    everything = sent_to_all(array, axis)
    return jnp.sum(everything, axis=0)


def joined_along(blocks, dim):
    blocks = jnp.moveaxis(blocks, 0, dim)
    shape = blocks.shape
    return blocks.reshape(*shape[:dim], shape[dim] * shape[dim + 1], *shape[dim + 2 :])


def gather_directly(array, axis, dim):
    return joined_along(sent_to_all(array, axis), dim)


def side_by_side(arrays, axis, dim, along):
    widths = [a.shape[along] for a in arrays]
    both = jnp.concatenate(arrays, axis=along)
    out = lax.all_gather(both, axis, axis=dim, tiled=True)
    return tuple(jnp.split(out, [sum(widths[:k]) for k in range(1, len(widths))], axis=along))


def build_mask(text_sees, tile_image, text_count):
    blocks_total = text_sees.shape[0]
    images_total = text_sees.shape[1]
    text_rows = lax.axis_index("txt") * text_count + jnp.arange(text_count, dtype=jnp.int32)
    text_block = text_rows // TBLK
    block_onehot = (
        text_block[:, None] == jnp.arange(blocks_total, dtype=jnp.int32)[None, :]
    ).astype(jnp.float32)
    row_sees = jnp.dot(block_onehot, text_sees.astype(jnp.float32))
    tile_onehot = (
        tile_image[:, None] == jnp.arange(images_total, dtype=jnp.int32)[None, :]
    ).astype(jnp.float32)
    tile_allowed = jnp.dot(row_sees, tile_onehot.T) > 0.5
    return jnp.repeat(tile_allowed, TILE, axis=1)


def shards(image_feats, key_weight, value_weight, queries, grad_out, tile_image, text_sees):
    key_part = jnp.dot(image_feats, key_weight, preferred_element_type=jnp.float32)
    value_part = jnp.dot(image_feats, value_weight, preferred_element_type=jnp.float32)
    key_own, value_own = in_one_piece((key_part, value_part), "head", 1, 0)
    keys, values = (
        lax.all_gather(key_own.astype(jnp.bfloat16), "txt", axis=0, tiled=True),
        lax.all_gather(value_own.astype(jnp.bfloat16), "txt", axis=0, tiled=True),
    )
    text_count = queries.shape[0]
    key_count = keys.shape[0]
    groups = keys.shape[1] // HD
    repeats = queries.shape[1] // (groups * HD)
    scale_factor = 1.0 / math.sqrt(HD)
    allowed = build_mask(text_sees, tile_image, text_count)
    query_heads = queries.reshape(text_count, groups, repeats, HD)
    grad_heads = grad_out.reshape(text_count, groups, repeats, HD)
    key_heads = keys.reshape(key_count, groups, HD)
    value_heads = values.reshape(key_count, groups, HD)
    scores = (
        jnp.einsum("tgrd,jgd->grtj", query_heads, key_heads, preferred_element_type=jnp.float32)
        * scale_factor
    )
    masked = jnp.where(allowed[None, None], scores, -1e30)
    row_max = of_everyone(jnp.max(masked, axis=-1), "img")
    weights = jnp.exp(masked - row_max[..., None]).astype(jnp.bfloat16)
    local_totals = (
        jnp.sum(weights, axis=-1, dtype=jnp.float32)
        .transpose(2, 0, 1)
        .reshape(text_count, groups * repeats)
    )
    numerator = jnp.einsum(
        "grtj,jgd->tgrd", weights, value_heads, preferred_element_type=jnp.float32
    )
    numerator = numerator.reshape(text_count, groups * repeats, HD)
    num_rows = summed_on_arrival(numerator, "img", 0)
    totals = of_everyone_2(local_totals, "img")
    share_rows = num_rows.shape[0]
    row_totals = lax.dynamic_slice_in_dim(totals, lax.axis_index("img") * share_rows, share_rows, 0)
    out_rows = (
        (num_rows / row_totals[..., None])
        .astype(jnp.bfloat16)
        .reshape(share_rows, groups * repeats * HD)
    )
    attn_out = gather_directly(out_rows, "img", 0)
    log_total = row_max + jnp.log(totals.reshape(text_count, groups, repeats).transpose(1, 2, 0))
    products = grad_out.astype(jnp.float32) * attn_out.astype(jnp.float32)
    row_delta = jnp.sum(products.reshape(text_count, groups, repeats, HD), axis=-1).transpose(
        1, 2, 0
    )
    key_grads = []
    value_grads = []
    for group_index in range(groups):
        probabilities = jnp.exp(masked[group_index] - log_total[group_index][..., None])
        grad_probs = jnp.einsum(
            "trd,jd->rtj",
            grad_heads[:, group_index],
            value_heads[:, group_index],
            preferred_element_type=jnp.float32,
        )
        grad_scores = (
            probabilities * (grad_probs - row_delta[group_index][..., None]) * scale_factor
        ).astype(jnp.bfloat16)
        value_grads.append(
            jnp.einsum(
                "rtj,trd->jd",
                probabilities.astype(jnp.bfloat16),
                grad_heads[:, group_index],
                preferred_element_type=jnp.float32,
            )
        )
        key_grads.append(
            jnp.einsum(
                "rtj,trd->jd",
                grad_scores,
                query_heads[:, group_index],
                preferred_element_type=jnp.float32,
            )
        )
    key_grad = jnp.concatenate(key_grads, axis=1)
    value_grad = jnp.concatenate(value_grads, axis=1)
    key_own_grad, value_own_grad = in_one_piece((key_grad, value_grad), "txt", 0, 1)
    key_all, value_all = side_by_side(
        (key_own_grad.astype(jnp.bfloat16), value_own_grad.astype(jnp.bfloat16)), "head", 1, 0
    )
    contract = (((1,), (1,)), ((), ()))
    grad_feats = lax.dot_general(key_all, key_weight, contract, preferred_element_type=jnp.float32)
    grad_feats = grad_feats + lax.dot_general(
        value_all, value_weight, contract, preferred_element_type=jnp.float32
    )
    return (attn_out, grad_feats.astype(jnp.bfloat16))


def solution(mesh):
    placed = (
        P(("img", "txt"), "head"),
        P("head", None),
        P("head", None),
        P("txt", "head"),
        P("txt", "head"),
        P("img"),
        P(),
    )
    return jax.shard_map(
        shards,
        mesh=mesh,
        in_specs=placed,
        out_specs=(P("txt", "head"), P(("img", "txt"), "head")),
        check_vma=False,
    )
```

profile of v0, /device:TPU:0, one launch (start us, length us, event | category | flops | bytes accessed | tf_op | source)
XLA Modules:
  0.0 227.6 jit_solution(16640007711787524154)
XLA Ops:
  0.7 1.5 copy-done
  2.2 3.5 %fusion.59 = f32[256,512]{1,0:T(8,128)S(1)} fusion(bf16[256,3840]{1,0:T(8,128)(2,1)S(1)} %copy-done, bf16[3840,512]{1,0:T(8,128)(2,1)} %param.8), kind=kOutput, calls=%fused_computation.72 | convolution fusion | flops 1006632960 | bytes 6422528 | tf_op jit(solution)/shard_map/dot_general | solution.py:81
  8.0 5.2 %all-to-all-start = ((f32[2,512,256]{2,1,0:T(8,128)}), f32[2,512,256]{2,1,0:T(8,128)S(1)}, u32[]{:S(2)}, u32[]{:S(2)}) async-start(f32[2,512,256]{2,1,0:T(8,128)} %bitcast.154), calls=%async_computation | async-start | bytes 2097152 | tf_op jit(solution)/shard_map/all_to_all | solution.py:19
  13.2 1.5 copy.82
  15.1 13.2 %all-to-all-done = f32[2,512,256]{2,1,0:T(8,128)S(1)} async-done(((f32[2,512,256]{2,1,0:T(8,128)}), f32[2,512,256]{2,1,0:T(8,128)S(1)}, u32[]{:S(2)}, u32[]{:S(2)}) %all-to-all-start) | async-done | bytes 1048608 | tf_op jit(solution)/shard_map/all_to_all | solution.py:19
  28.4 13.9 %all_gather.10 = bf16[1024,256]{1,0:T(8,128)(2,1)S(1)} all-gather(bf16[256,256]{1,0:T(8,128)(2,1)S(1)} %get-tuple-element.6), channel_id=1, replica_groups=mesh['img'=16,'head'=2,'txt'=4] {'txt'}, dimensions={0}, use_global_device_ids=true | all-gather | bytes 655360 | tf_op jit(solution)/shard_map/all_gather | solution.py:85
  42.6 7.3 %fusion.58 = (f32[2,8,256]{2,1,0:T(8,128)S(1)}, f32[2,8,256,1024]{2,3,1,0:T(8,128)}) fusion(bf16[1024,2,128,1]{0,2,3,1:T(8,128)(2,1)S(1)} %bitcast.166, bf16[256,2,8,128]{0,3,2,1:T(8,128)(2,1)S(1)} %bitcast.161, pred[256,1024]{0,1:T(8,128)(4,1)S(1)} %bitcast.164), kind=kOutput, calls=%fused_computation.71 | convolution fusion | flops 1086320640 | bytes 18628608 | tf_op jit(solution)/shard_map/tgrd,jgd->grtj/dot_general | solution.py:99
  50.6 4.9 %all-to-all-start.1 = ((f32[16,2,8,256]{3,2,1,0:T(8,128)}), f32[16,2,8,256]{3,2,1,0:T(8,128)S(1)}, u32[]{:S(2)}, u32[]{:S(2)}) async-start(f32[16,2,8,256]{3,2,1,0:T(8,128)} %broadcast_in_dim.36), calls=%async_computation.1 | async-start | bytes 524288 | tf_op jit(solution)/shard_map/all_to_all | solution.py:34
  55.4 12.9 %all_gather.9 = bf16[1024,256]{1,0:T(8,128)(2,1)S(1)} all-gather(bf16[256,256]{1,0:T(8,128)(2,1)S(1)} %get-tuple-element.7), channel_id=1, replica_groups=mesh['img'=16,'head'=2,'txt'=4] {'txt'}, dimensions={0}, use_global_device_ids=true | all-gather | bytes 655360 | tf_op jit(solution)/shard_map/all_gather | solution.py:86
  68.6 8.0 %convert_reduce_fusion = f32[2,8,256]{2,1,0:T(8,128)S(1)} fusion(f32[2,8,256,1024]{2,3,1,0:T(8,128)} %get-tuple-element.11, f32[2,8,256]{2,1,0:T(8,128)S(1)} %reduce_max.19), kind=kLoop, calls=%fused_computation.1 | loop fusion | flops 16773120 | bytes 16809984 | tf_op jit(solution)/shard_map/reduce_sum | solution.py:106
  77.3 5.5 %all-to-all-start.3 = ((f32[16,256,16]{1,2,0:T(8,128)}), f32[16,256,16]{1,2,0:T(8,128)S(1)}, u32[]{:S(2)}, u32[]{:S(2)}) async-start(f32[16,256,16]{1,2,0:T(8,128)} %broadcast_in_dim.37), calls=%async_computation.3 | async-start | bytes 524288 | tf_op jit(solution)/shard_map/all_to_all | solution.py:34
  82.9 10.0 %fusion.26 = f32[256,2,8,128]{0,3,2,1:T(8,128)} fusion(bf16[1024,2,128,1]{0,2,3,1:T(8,128)(2,1)S(1)} %bitcast.167, f32[2,8,256,1024]{2,3,1,0:T(8,128)} %get-tuple-element.11, f32[2,8,256]{2,1,0:T(8,128)S(1)} %reduce_max.19), kind=kOutput, calls=%fused_computation.31 | convolution fusion | flops 1082130432 | bytes 19415040 | tf_op jit(solution)/shard_map/grtj,jgd->tgrd/dot_general | solution.py:110
  92.9 3.2 %copy.86 = f32[256,2,8,128]{3,2,1,0:T(8,128)} copy(f32[256,2,8,128]{0,3,2,1:T(8,128)} %fusion.26) | data formatting | bytes 4194304 | tf_op jit(solution)/shard_map/grtj,jgd->tgrd/transpose | solution.py:110
  96.1 5.8 %all-to-all-start.2 = ((f32[16,16,16,128]{3,2,1,0:T(8,128)}), f32[16,16,16,128]{3,2,1,0:T(8,128)}, u32[]{:S(2)}, u32[]{:S(2)}) async-start(f32[16,16,16,128]{3,2,1,0:T(8,128)} %bitcast.158), calls=%async_computation.2 | async-start | bytes 4194304 | tf_op jit(solution)/shard_map/all_to_all | solution.py:19
  103.4 26.6 %all-to-all-done.2 = f32[16,16,16,128]{3,2,1,0:T(8,128)} async-done(((f32[16,16,16,128]{3,2,1,0:T(8,128)}), f32[16,16,16,128]{3,2,1,0:T(8,128)}, u32[]{:S(2)}, u32[]{:S(2)}) %all-to-all-start.2) | async-done | bytes 2097184 | tf_op jit(solution)/shard_map/all_to_all | solution.py:19
  130.0 1.7 reduce_sum.55
  132.9 4.6 %all-to-all-start.4 = ((bf16[16,16,2048]{2,1,0:T(8,128)(2,1)}), bf16[16,16,2048]{2,1,0:T(8,128)(2,1)S(1)}, u32[]{:S(2)}, u32[]{:S(2)}) async-start(bf16[16,16,2048]{2,1,0:T(8,128)(2,1)} %broadcast_in_dim.38), calls=%async_computation.4 | async-start | bytes 2097152 | tf_op jit(solution)/shard_map/all_to_all | solution.py:34
  137.5 5.9 %fusion.33 = f32[1024,128]{0,1:T(8,128)} fusion(f32[2,8,256,1024]{2,3,1,0:T(8,128)} %get-tuple-element.11, f32[8,256]{1,0:T(8,128)S(1)} %get-tuple-element.8, bf16[256,2,8,128]{0,3,2,1:T(8,128)(2,1)} %bitcast.171), kind=kOutput, calls=%fused_computation.34 | convolution fusion | flops 541065216 | bytes 9445376 | tf_op jit(solution)/shard_map/rtj,trd->jd/dot_general | solution.py:143
  143.4 5.7 %fusion.36 = f32[1024,128]{0,1:T(8,128)} fusion(f32[2,8,256,1024]{2,3,1,0:T(8,128)} %get-tuple-element.11, f32[8,256]{1,0:T(8,128)S(1)} %get-tuple-element.9, bf16[256,2,8,128]{0,3,2,1:T(8,128)(2,1)S(1)} %bitcast.174), kind=kOutput, calls=%fused_computation.35 | convolution fusion | flops 541065216 | bytes 9445376 | tf_op jit(solution)/shard_map/rtj,trd->jd/dot_general | solution.py:143
  149.1 4.9 %all-to-all-done.4 = bf16[16,16,2048]{2,1,0:T(8,128)(2,1)S(1)} async-done(((bf16[16,16,2048]{2,1,0:T(8,128)(2,1)}), bf16[16,16,2048]{2,1,0:T(8,128)(2,1)S(1)}, u32[]{:S(2)}, u32[]{:S(2)}) %all-to-all-start.4) | async-done | bytes 1048608 | tf_op jit(solution)/shard_map/all_to_all | solution.py:34
  154.0 1.6 multiply_bitcast_fusion
  155.6 1.7 copy.126
  157.3 2.4 %reduce_sum.58 = f32[256,2,8]{2,1,0:T(2,128)S(1)} reduce(f32[256,2,8,128]{3,2,1,0:T(8,128)} %bitcast.157, f32[]{:T(128)} %constant.14.clone.1), dimensions={3}, to_apply=%region_6.7 | reduce | flops 520192 | bytes 2113540 | tf_op jit(solution)/shard_map/reduce_sum | solution.py:126
  160.0 7.6 %fusion.30 = f32[1024,128]{0,1:T(8,128)} fusion(f32[2,8,256,1024]{2,3,1,0:T(8,128)} %get-tuple-element.11, f32[8,256]{1,0:T(8,128)S(1)} %copy.91, f32[8,256]{1,0:T(8,128)S(1)} %get-tuple-element.8, bf16[256,2,8,128]{0,3,2,1:T(8,128)(2,1)S(1)} %bitcast.162, bf16[256,2,8,128]{0,3,2,1:T(8,128)(2,1)} %bitcast.172, bf16[1024,2,128]{0,2,1:T(8,128)(2,1)S(1)} %bitcast.168), kind=kOutput, calls=%fused_computation.33 | convolution fusion | flops 1084227584 | bytes 10240000 | tf_op jit(solution)/shard_map/rtj,trd->jd/dot_general | solution.py:151
  167.5 7.6 %fusion.27 = f32[1024,128]{0,1:T(8,128)} fusion(f32[2,8,256,1024]{2,3,1,0:T(8,128)} %get-tuple-element.11, f32[8,256]{1,0:T(8,128)S(1)} %copy.95, f32[8,256]{1,0:T(8,128)S(1)} %get-tuple-element.9, bf16[256,2,8,128]{0,3,2,1:T(8,128)(2,1)S(1)} %bitcast.163, bf16[256,2,8,128]{0,3,2,1:T(8,128)(2,1)} %bitcast.173, bf16[1024,2,128]{0,2,1:T(8,128)(2,1)S(1)} %bitcast.169), kind=kOutput, calls=%fused_computation.32 | convolution fusion | flops 1084227584 | bytes 10240000 | tf_op jit(solution)/shard_map/rtj,trd->jd/dot_general | solution.py:151
  175.1 1.6 pad_maximum_fusion
  178.2 4.4 %all-to-all-start.5 = ((f32[4,256,512]{1,2,0:T(8,128)}), f32[4,256,512]{1,2,0:T(8,128)}, u32[]{:S(2)}, u32[]{:S(2)}) async-start(f32[4,256,512]{1,2,0:T(8,128)} %bitcast.159), calls=%async_computation.5 | async-start | bytes 4194304 | tf_op jit(solution)/shard_map/all_to_all | solution.py:19
  182.6 26.6 %all-to-all-done.5 = f32[4,256,512]{1,2,0:T(8,128)} async-done(((f32[4,256,512]{1,2,0:T(8,128)}), f32[4,256,512]{1,2,0:T(8,128)}, u32[]{:S(2)}, u32[]{:S(2)}) %all-to-all-start.5) | async-done | bytes 2097184 | tf_op jit(solution)/shard_map/all_to_all | solution.py:19
  209.2 1.7 reduce_sum.59
  211.0 9.5 %all_gather.11 = bf16[512,512]{0,1:T(8,128)(2,1)S(1)} all-gather(bf16[512,256]{0,1:T(8,128)(2,1)S(1)} %pad_maximum_fusion.2), channel_id=1, replica_groups=mesh['img'=16,'head'=2,'txt'=4] {'head'}, dimensions={1}, use_global_device_ids=true | all-gather | bytes 786432 | tf_op jit(solution)/shard_map/all_gather | solution.py:60
  220.6 3.5 %fusion.46 = f32[256,3840]{1,0:T(8,128)S(1)} fusion(bf16[3840,512]{1,0:T(8,128)(2,1)} %param.8, bf16[512,512]{0,1:T(8,128)(2,1)S(1)} %all_gather.11), kind=kOutput, calls=%fused_computation.46 | convolution fusion | flops 1006632960 | bytes 8126464 | tf_op jit(solution)/shard_map/dot_general | solution.py:165
  224.1 2.5 %fusion.12 = bf16[256,3840]{1,0:T(8,128)(2,1)} fusion(f32[256,3840]{1,0:T(8,128)S(1)} %fusion.46, bf16[3840,512]{1,0:T(8,128)(2,1)S(1)} %copy-done.4, bf16[512,512]{0,1:T(8,128)(2,1)S(1)} %all_gather.11), kind=kOutput, calls=%fused_computation.20 | convolution fusion | flops 1008599040 | bytes 10092544 | tf_op jit(solution)/shard_map/dot_general | solution.py:166
  (48 shorter events, 10.3 us)
Async XLA Ops:
  0.6 1.6 copy-start
  0.6 5.0 %copy-start.3 = (bf16[3840,512]{1,0:T(8,128)(2,1)S(1)}, bf16[3840,512]{1,0:T(8,128)(2,1)}, u32[]{:S(2)}) copy-start(bf16[3840,512]{1,0:T(8,128)(2,1)} %param.9) | copy-start | bytes 11796484
  6.8 7.9 %copy-start.7 = (s32[8,8]{1,0:T(8,128)S(1)}, s32[8,8]{1,0:T(8,128)}, u32[]{:S(2)}) copy-start(s32[8,8]{1,0:T(8,128)} %param.13) | copy-start | bytes 772
  6.9 7.9 %copy-start.8 = (s32[8]{0:T(128)S(1)}, s32[8]{0:T(128)}, u32[]{:S(2)}) copy-start(s32[8]{0:T(128)} %param.12) | copy-start | bytes 100
  8.0 20.3 %all-to-all-start = ((f32[2,512,256]{2,1,0:T(8,128)}), f32[2,512,256]{2,1,0:T(8,128)S(1)}, u32[]{:S(2)}, u32[]{:S(2)}) async-start(f32[2,512,256]{2,1,0:T(8,128)} %bitcast.154), calls=%async_computation | async-start | bytes 2097152 | tf_op jit(solution)/shard_map/all_to_all | solution.py:19
  50.6 18.0 %all-to-all-start.1 = ((f32[16,2,8,256]{3,2,1,0:T(8,128)}), f32[16,2,8,256]{3,2,1,0:T(8,128)S(1)}, u32[]{:S(2)}, u32[]{:S(2)}) async-start(f32[16,2,8,256]{3,2,1,0:T(8,128)} %broadcast_in_dim.36), calls=%async_computation.1 | async-start | bytes 524288 | tf_op jit(solution)/shard_map/all_to_all | solution.py:34
  77.3 18.7 %all-to-all-start.3 = ((f32[16,256,16]{1,2,0:T(8,128)}), f32[16,256,16]{1,2,0:T(8,128)S(1)}, u32[]{:S(2)}, u32[]{:S(2)}) async-start(f32[16,256,16]{1,2,0:T(8,128)} %broadcast_in_dim.37), calls=%async_computation.3 | async-start | bytes 524288 | tf_op jit(solution)/shard_map/all_to_all | solution.py:34
  92.9 9.0 %copy-start.2 = (bf16[256,2048]{1,0:T(8,128)(2,1)S(1)}, bf16[256,2048]{1,0:T(8,128)(2,1)}, u32[]{:S(2)}) copy-start(bf16[256,2048]{1,0:T(8,128)(2,1)} %param.11) | copy-start | bytes 3145732
  96.1 33.9 %all-to-all-start.2 = ((f32[16,16,16,128]{3,2,1,0:T(8,128)}), f32[16,16,16,128]{3,2,1,0:T(8,128)}, u32[]{:S(2)}, u32[]{:S(2)}) async-start(f32[16,16,16,128]{3,2,1,0:T(8,128)} %bitcast.158), calls=%async_computation.2 | async-start | bytes 4194304 | tf_op jit(solution)/shard_map/all_to_all | solution.py:19
  132.9 21.0 %all-to-all-start.4 = ((bf16[16,16,2048]{2,1,0:T(8,128)(2,1)}), bf16[16,16,2048]{2,1,0:T(8,128)(2,1)S(1)}, u32[]{:S(2)}, u32[]{:S(2)}) async-start(bf16[16,16,2048]{2,1,0:T(8,128)(2,1)} %broadcast_in_dim.38), calls=%async_computation.4 | async-start | bytes 2097152 | tf_op jit(solution)/shard_map/all_to_all | solution.py:34
  137.5 5.9 %copy-start.5 = (bf16[256,2048]{0,1:T(8,128)(2,1)S(1)}, bf16[256,2048]{0,1:T(8,128)(2,1)}, u32[]{:S(2)}) copy-start(bf16[256,2048]{0,1:T(8,128)(2,1)} %copy.88) | copy-start | bytes 3145732
  167.5 7.6 %copy-start.6 = (f32[1024,128]{0,1:T(8,128)S(1)}, f32[1024,128]{0,1:T(8,128)}, u32[]{:S(2)}) copy-start(f32[1024,128]{0,1:T(8,128)} %fusion.33) | copy-start | bytes 1572868
  178.2 31.1 %all-to-all-start.5 = ((f32[4,256,512]{1,2,0:T(8,128)}), f32[4,256,512]{1,2,0:T(8,128)}, u32[]{:S(2)}, u32[]{:S(2)}) async-start(f32[4,256,512]{1,2,0:T(8,128)} %bitcast.159), calls=%async_computation.5 | async-start | bytes 4194304 | tf_op jit(solution)/shard_map/all_to_all | solution.py:19
  220.5 3.5 %copy-start.4 = (bf16[3840,512]{1,0:T(8,128)(2,1)S(1)}, bf16[3840,512]{1,0:T(8,128)(2,1)}, u32[]{:S(2)}) copy-start(bf16[3840,512]{1,0:T(8,128)(2,1)} %param.9) | copy-start | bytes 11796484
  220.6 7.0 %copy-start.1 = (bf16[256,3840]{1,0:T(8,128)(2,1)S(1)}, bf16[256,3840]{1,0:T(8,128)(2,1)}, u32[]{:S(2)}) copy-start(bf16[256,3840]{1,0:T(8,128)(2,1)} %param.7) | copy-start | bytes 5898244
where the time goes:
time: 229 us; the launch traced here: 228 us
  waiting for transfers between devices  71.3 us (31%)
  matrix products  55 us (24%)
  blocking collectives  36.3 us (16%)
  starting transfers between devices  30.4 us (13%)
  other arithmetic  17.3 us (8%)
  local copies, waits for them, and re-layouts  16.3 us (7%)
    all_to_all x3, waiting for transfers between devices, summed_on_arrival(): lax.all_to_all(in_blocks(array, dim, length), axis, 0, 0, tiled=True)  66.5 us
    all_to_all x3, starting transfers between devices, summed_on_arrival(): lax.all_to_all(in_blocks(array, dim, length), axis, 0, 0, tiled=True)  15.4 us
    dot_general x2, matrix products, shards(): jnp.einsum('rtj,trd->jd', grad_scores, query_heads[:, group_index], prefe...  15.1 us
    all_to_all x3, starting transfers between devices, sent_to_all(): return lax.all_to_all(copies, axis, split_axis=0, concat_axis=0, tiled=True)  15 us
    all_gather x1, blocking collectives, shards(): lax.all_gather(key_own.astype(jnp.bfloat16), 'txt', axis=0, tiled=True)  13.9 us
    all_gather x1, blocking collectives, shards(): lax.all_gather(value_own.astype(jnp.bfloat16), 'txt', axis=0, tiled=True)  12.9 us
    dot_general x2, matrix products, shards(): jnp.einsum('rtj,trd->jd', probabilities.astype(jnp.bfloat16), grad_heads[...  11.6 us
    dot_general x1, matrix products, shards(): jnp.einsum('grtj,jgd->tgrd', weights, value_heads, preferred_element_type...  10 us
  transfers between devices with their start and end apart: 6, of which 4 were waited for; matrix products, arithmetic and copies ran while one was open for 12% of the time, Pallas kernels for 0%

commit v1 on v0

--- a/solution.py
+++ b/solution.py
@@ -7,6 +7,34 @@
 HD = 128
 TILE = 128
 TBLK = 128
+
+
+def recast_racks(my_data, join_dim):
+    device_axis = "txt"
+    newest = lax.psum(1, axis_name=device_axis)
+    v1, far_arr, y = (newest, lax.axis_index(device_axis), my_data.shape[join_dim])
+    pieces_in = tuple(
+        (to_i * v1 if ii == join_dim else to_i for ii, to_i in enumerate(my_data.shape))
+    )
+    local_now = lax.dynamic_update_slice_in_dim(
+        jnp.zeros(pieces_in, my_data.dtype), my_data, far_arr * y, axis=join_dim
+    )
+    tmp = h_now = my_data
+    it = 1
+    while it < v1 // 2 + 1:
+        upper = tuple(((ii, (ii + 1) % v1) for ii in range(v1)))
+        tmp = lax.ppermute(tmp, axis_name=device_axis, perm=upper)
+        local_now = lax.dynamic_update_slice_in_dim(
+            local_now, tmp, (far_arr - it) % v1 * y, axis=join_dim
+        )
+        if 2 * it < v1:
+            s_next = tuple(((ii, (ii - 1) % v1) for ii in range(v1)))
+            h_now = lax.ppermute(h_now, axis_name=device_axis, perm=s_next)
+            local_now = lax.dynamic_update_slice_in_dim(
+                local_now, h_now, (far_arr + it) % v1 * y, axis=join_dim
+            )
+        it += 1
+    return local_now
 
 
 def in_blocks(array, dim, length):
@@ -82,7 +110,7 @@
     value_part = jnp.dot(image_feats, value_weight, preferred_element_type=jnp.float32)
     key_own, value_own = in_one_piece((key_part, value_part), "head", 1, 0)
     keys, values = (
-        lax.all_gather(key_own.astype(jnp.bfloat16), "txt", axis=0, tiled=True),
+        recast_racks(key_own.astype(jnp.bfloat16), 0),
         lax.all_gather(value_own.astype(jnp.bfloat16), "txt", axis=0, tiled=True),
     )
     text_count = queries.shape[0]

time: 229 us -> 228 us (level)
  blocking collectives: 36.3 us -> 22.7 us
  waiting for transfers between devices: 71.3 us -> 80.6 us
  starting transfers between devices: 30.4 us -> 34.7 us
    all_gather x1 -> x0, blocking collectives: 13.9 us -> none  [shards(): lax.all_gather(key_own.astype(jnp.bfloat16), 'txt', axis=0, tiled=True)]
    ppermute x0 -> x3, waiting for transfers between devices: none -> 7.45 us  [the longest x2 6.57 us: recast_racks(): tmp = lax.ppermute(tmp, axis_name=device_axis, perm=upper)]
    ppermute x0 -> x3, starting transfers between devices: none -> 3.81 us  [the longest x2 2.08 us: recast_racks(): tmp = lax.ppermute(tmp, axis_name=device_axis, perm=upper)]
    unnamed x23 -> x25, local copies, waits for them, and re-layouts: 7.06 us -> 6.13 us
  transfers between devices with their start and end apart: 6 -> 9, of which waited for: 4 -> 7; matrix products, arithmetic and copies ran while one was open for 12% -> 12% of each run, Pallas kernels for 0% -> 0%
where the time goes in v1:
time: 228 us; the launch traced here: 227 us
  waiting for transfers between devices  80.6 us (35%)
  matrix products  55 us (24%)
  starting transfers between devices  34.7 us (15%)
  blocking collectives  22.7 us (10%)
  other arithmetic  17.3 us (8%)
  local copies, waits for them, and re-layouts  15.7 us (7%)
    all_to_all x3, waiting for transfers between devices, summed_on_arrival(): lax.all_to_all(in_blocks(array, dim, length), axis, 0, 0, tiled=True)  68.3 us
    all_to_all x3, starting transfers between devices, sent_to_all(): return lax.all_to_all(copies, axis, split_axis=0, concat_axis=0, tiled=True)  15.5 us
    all_to_all x3, starting transfers between devices, summed_on_arrival(): lax.all_to_all(in_blocks(array, dim, length), axis, 0, 0, tiled=True)  15.4 us
    dot_general x2, matrix products, shards(): jnp.einsum('rtj,trd->jd', grad_scores, query_heads[:, group_index], prefe...  15.1 us
    all_gather x1, blocking collectives, shards(): lax.all_gather(value_own.astype(jnp.bfloat16), 'txt', axis=0, tiled=True)  13.2 us
    dot_general x2, matrix products, shards(): jnp.einsum('rtj,trd->jd', probabilities.astype(jnp.bfloat16), grad_heads[...  11.6 us
    dot_general x1, matrix products, shards(): jnp.einsum('grtj,jgd->tgrd', weights, value_heads, preferred_element_type...  10 us
    all_gather x1, blocking collectives, side_by_side(): out = lax.all_gather(both, axis, axis=dim, tiled=True)  9.52 us
  transfers between devices with their start and end apart: 9, of which 7 were waited for; matrix products, arithmetic and copies ran while one was open for 12% of the time, Pallas kernels for 0%

profile of v1, /device:TPU:0, one launch (start us, length us, event | category | flops | bytes accessed | tf_op | source)
XLA Modules:
  0.0 227.1 jit_solution(4943375516449773845)
XLA Ops:
  2.2 3.5 %fusion.59 = f32[256,512]{1,0:T(8,128)S(1)} fusion(bf16[256,3840]{1,0:T(8,128)(2,1)S(1)} %copy-done, bf16[3840,512]{1,0:T(8,128)(2,1)} %param.8), kind=kOutput, calls=%fused_computation.76 | convolution fusion | flops 1006632960 | bytes 6422528 | tf_op jit(solution)/shard_map/dot_general | solution.py:109
  8.0 5.2 %all-to-all-start = ((f32[2,512,256]{2,1,0:T(8,128)}), f32[2,512,256]{2,1,0:T(8,128)S(1)}, u32[]{:S(2)}, u32[]{:S(2)}) async-start(f32[2,512,256]{2,1,0:T(8,128)} %bitcast.154), calls=%async_computation | async-start | bytes 2097152 | tf_op jit(solution)/shard_map/all_to_all | solution.py:47
  13.3 15.1 %all-to-all-done = f32[2,512,256]{2,1,0:T(8,128)S(1)} async-done(((f32[2,512,256]{2,1,0:T(8,128)}), f32[2,512,256]{2,1,0:T(8,128)S(1)}, u32[]{:S(2)}, u32[]{:S(2)}) %all-to-all-start) | async-done | bytes 1048608 | tf_op jit(solution)/shard_map/all_to_all | solution.py:47
  28.4 1.6 collective-permute-start
  31.1 1.7 collective-permute-start.1
  32.9 1.8 collective-permute-done
  36.3 4.8 %collective-permute-done.2 = bf16[256,256]{1,0:T(8,128)(2,1)S(1)} collective-permute-done((bf16[256,256]{1,0:T(8,128)(2,1)S(1)}, bf16[256,256]{1,0:T(8,128)(2,1)S(1)}, u32[]{:S(2)}, u32[]{:S(2)}) %collective-permute-start.2) | collective-permute-done | bytes 131104 | tf_op jit(solution)/shard_map/ppermute | solution.py:26
  41.3 7.3 %fusion.58 = (f32[2,8,256]{2,1,0:T(8,128)S(1)}, f32[2,8,256,1024]{2,3,1,0:T(8,128)}) fusion(bf16[1024,2,128,1]{0,2,3,1:T(8,128)(2,1)S(1)} %bitcast.166, bf16[256,2,8,128]{0,3,2,1:T(8,128)(2,1)S(1)} %bitcast.161, pred[256,1024]{0,1:T(8,128)(4,1)S(1)} %bitcast.164), kind=kOutput, calls=%fused_computation.75 | convolution fusion | flops 1086320640 | bytes 18628608 | tf_op jit(solution)/shard_map/tgrd,jgd->grtj/dot_general | solution.py:127
  49.2 4.9 %all-to-all-start.1 = ((f32[16,2,8,256]{3,2,1,0:T(8,128)}), f32[16,2,8,256]{3,2,1,0:T(8,128)S(1)}, u32[]{:S(2)}, u32[]{:S(2)}) async-start(f32[16,2,8,256]{3,2,1,0:T(8,128)} %broadcast_in_dim.40), calls=%async_computation.1 | async-start | bytes 524288 | tf_op jit(solution)/shard_map/all_to_all | solution.py:62
  54.1 13.2 %all_gather.6 = bf16[1024,256]{1,0:T(8,128)(2,1)S(1)} all-gather(bf16[256,256]{1,0:T(8,128)(2,1)S(1)} %get-tuple-element.7), channel_id=1, replica_groups=mesh['img'=16,'head'=2,'txt'=4] {'txt'}, dimensions={0}, use_global_device_ids=true | all-gather | bytes 655360 | tf_op jit(solution)/shard_map/all_gather | solution.py:114
  67.6 8.0 %convert_reduce_fusion = f32[2,8,256]{2,1,0:T(8,128)S(1)} fusion(f32[2,8,256,1024]{2,3,1,0:T(8,128)} %get-tuple-element.11, f32[2,8,256]{2,1,0:T(8,128)S(1)} %reduce_max.19), kind=kLoop, calls=%fused_computation.1 | loop fusion | flops 16773120 | bytes 16809984 | tf_op jit(solution)/shard_map/reduce_sum | solution.py:134
  76.3 5.9 %all-to-all-start.3 = ((f32[16,256,16]{1,2,0:T(8,128)}), f32[16,256,16]{1,2,0:T(8,128)S(1)}, u32[]{:S(2)}, u32[]{:S(2)}) async-start(f32[16,256,16]{1,2,0:T(8,128)} %broadcast_in_dim.41), calls=%async_computation.3 | async-start | bytes 524288 | tf_op jit(solution)/shard_map/all_to_all | solution.py:62
  82.2 10.0 %fusion.26 = f32[256,2,8,128]{0,3,2,1:T(8,128)} fusion(bf16[1024,2,128,1]{0,2,3,1:T(8,128)(2,1)S(1)} %bitcast.167, f32[2,8,256,1024]{2,3,1,0:T(8,128)} %get-tuple-element.11, f32[2,8,256]{2,1,0:T(8,128)S(1)} %reduce_max.19), kind=kOutput, calls=%fused_computation.31 | convolution fusion | flops 1082130432 | bytes 19415040 | tf_op jit(solution)/shard_map/grtj,jgd->tgrd/dot_general | solution.py:138
  92.2 3.2 %copy.95 = f32[256,2,8,128]{3,2,1,0:T(8,128)} copy(f32[256,2,8,128]{0,3,2,1:T(8,128)} %fusion.26) | data formatting | bytes 4194304 | tf_op jit(solution)/shard_map/grtj,jgd->tgrd/transpose | solution.py:138
  95.4 5.8 %all-to-all-start.2 = ((f32[16,16,16,128]{3,2,1,0:T(8,128)}), f32[16,16,16,128]{3,2,1,0:T(8,128)}, u32[]{:S(2)}, u32[]{:S(2)}) async-start(f32[16,16,16,128]{3,2,1,0:T(8,128)} %bitcast.158), calls=%async_computation.2 | async-start | bytes 4194304 | tf_op jit(solution)/shard_map/all_to_all | solution.py:47
  102.7 26.6 %all-to-all-done.2 = f32[16,16,16,128]{3,2,1,0:T(8,128)} async-done(((f32[16,16,16,128]{3,2,1,0:T(8,128)}), f32[16,16,16,128]{3,2,1,0:T(8,128)}, u32[]{:S(2)}, u32[]{:S(2)}) %all-to-all-start.2) | async-done | bytes 2097184 | tf_op jit(solution)/shard_map/all_to_all | solution.py:47
  129.3 1.7 reduce_sum.55
  132.2 4.7 %all-to-all-start.4 = ((bf16[16,16,2048]{2,1,0:T(8,128)(2,1)}), bf16[16,16,2048]{2,1,0:T(8,128)(2,1)S(1)}, u32[]{:S(2)}, u32[]{:S(2)}) async-start(bf16[16,16,2048]{2,1,0:T(8,128)(2,1)} %broadcast_in_dim.42), calls=%async_computation.4 | async-start | bytes 2097152 | tf_op jit(solution)/shard_map/all_to_all | solution.py:62
  137.0 5.9 %fusion.33 = f32[1024,128]{0,1:T(8,128)} fusion(f32[2,8,256,1024]{2,3,1,0:T(8,128)} %get-tuple-element.11, f32[8,256]{1,0:T(8,128)S(1)} %get-tuple-element.8, bf16[256,2,8,128]{0,3,2,1:T(8,128)(2,1)} %bitcast.171), kind=kOutput, calls=%fused_computation.34 | convolution fusion | flops 541065216 | bytes 9445376 | tf_op jit(solution)/shard_map/rtj,trd->jd/dot_general | solution.py:171
  142.9 5.7 %fusion.36 = f32[1024,128]{0,1:T(8,128)} fusion(f32[2,8,256,1024]{2,3,1,0:T(8,128)} %get-tuple-element.11, f32[8,256]{1,0:T(8,128)S(1)} %get-tuple-element.9, bf16[256,2,8,128]{0,3,2,1:T(8,128)(2,1)S(1)} %bitcast.174), kind=kOutput, calls=%fused_computation.35 | convolution fusion | flops 541065216 | bytes 9445376 | tf_op jit(solution)/shard_map/rtj,trd->jd/dot_general | solution.py:171
  148.6 4.9 %all-to-all-done.4 = bf16[16,16,2048]{2,1,0:T(8,128)(2,1)S(1)} async-done(((bf16[16,16,2048]{2,1,0:T(8,128)(2,1)}), bf16[16,16,2048]{2,1,0:T(8,128)(2,1)S(1)}, u32[]{:S(2)}, u32[]{:S(2)}) %all-to-all-start.4) | async-done | bytes 1048608 | tf_op jit(solution)/shard_map/all_to_all | solution.py:62
  153.5 1.6 multiply_bitcast_fusion
  155.0 1.7 copy.135
  156.8 2.4 %reduce_sum.58 = f32[256,2,8]{2,1,0:T(2,128)S(1)} reduce(f32[256,2,8,128]{3,2,1,0:T(8,128)} %bitcast.157, f32[]{:T(128)} %constant.51.clone.1), dimensions={3}, to_apply=%region_6.7 | reduce | flops 520192 | bytes 2113540 | tf_op jit(solution)/shard_map/reduce_sum | solution.py:154
  159.5 7.6 %fusion.30 = f32[1024,128]{0,1:T(8,128)} fusion(f32[2,8,256,1024]{2,3,1,0:T(8,128)} %get-tuple-element.11, f32[8,256]{1,0:T(8,128)S(1)} %copy.100, f32[8,256]{1,0:T(8,128)S(1)} %get-tuple-element.8, bf16[256,2,8,128]{0,3,2,1:T(8,128)(2,1)S(1)} %bitcast.162, bf16[256,2,8,128]{0,3,2,1:T(8,128)(2,1)} %bitcast.172, bf16[1024,2,128]{0,2,1:T(8,128)(2,1)S(1)} %bitcast.168), kind=kOutput, calls=%fused_computation.33 | convolution fusion | flops 1084227584 | bytes 10240000 | tf_op jit(solution)/shard_map/rtj,trd->jd/dot_general | solution.py:179
  167.0 7.6 %fusion.27 = f32[1024,128]{0,1:T(8,128)} fusion(f32[2,8,256,1024]{2,3,1,0:T(8,128)} %get-tuple-element.11, f32[8,256]{1,0:T(8,128)S(1)} %copy.104, f32[8,256]{1,0:T(8,128)S(1)} %get-tuple-element.9, bf16[256,2,8,128]{0,3,2,1:T(8,128)(2,1)S(1)} %bitcast.163, bf16[256,2,8,128]{0,3,2,1:T(8,128)(2,1)} %bitcast.173, bf16[1024,2,128]{0,2,1:T(8,128)(2,1)S(1)} %bitcast.169), kind=kOutput, calls=%fused_computation.32 | convolution fusion | flops 1084227584 | bytes 10240000 | tf_op jit(solution)/shard_map/rtj,trd->jd/dot_general | solution.py:179
  177.7 4.4 %all-to-all-start.5 = ((f32[4,256,512]{1,2,0:T(8,128)}), f32[4,256,512]{1,2,0:T(8,128)}, u32[]{:S(2)}, u32[]{:S(2)}) async-start(f32[4,256,512]{1,2,0:T(8,128)} %bitcast.159), calls=%async_computation.5 | async-start | bytes 4194304 | tf_op jit(solution)/shard_map/all_to_all | solution.py:47
  182.1 26.6 %all-to-all-done.5 = f32[4,256,512]{1,2,0:T(8,128)} async-done(((f32[4,256,512]{1,2,0:T(8,128)}), f32[4,256,512]{1,2,0:T(8,128)}, u32[]{:S(2)}, u32[]{:S(2)}) %all-to-all-start.5) | async-done | bytes 2097184 | tf_op jit(solution)/shard_map/all_to_all | solution.py:47
  208.7 1.7 reduce_sum.59
  210.5 9.5 %all_gather.7 = bf16[512,512]{0,1:T(8,128)(2,1)S(1)} all-gather(bf16[512,256]{0,1:T(8,128)(2,1)S(1)} %pad_maximum_fusion.2), channel_id=1, replica_groups=mesh['img'=16,'head'=2,'txt'=4] {'head'}, dimensions={1}, use_global_device_ids=true | all-gather | bytes 786432 | tf_op jit(solution)/shard_map/all_gather | solution.py:88
  220.1 3.5 %fusion.46 = f32[256,3840]{1,0:T(8,128)S(1)} fusion(bf16[3840,512]{1,0:T(8,128)(2,1)} %param.8, bf16[512,512]{0,1:T(8,128)(2,1)S(1)} %all_gather.7), kind=kOutput, calls=%fused_computation.46 | convolution fusion | flops 1006632960 | bytes 8126464 | tf_op jit(solution)/shard_map/dot_general | solution.py:193
  223.6 2.5 %fusion.12 = bf16[256,3840]{1,0:T(8,128)(2,1)} fusion(f32[256,3840]{1,0:T(8,128)S(1)} %fusion.46, bf16[3840,512]{1,0:T(8,128)(2,1)S(1)} %copy-done.4, bf16[512,512]{0,1:T(8,128)(2,1)S(1)} %all_gather.7), kind=kOutput, calls=%fused_computation.20 | convolution fusion | flops 1008599040 | bytes 10092544 | tf_op jit(solution)/shard_map/dot_general | solution.py:194
  (63 shorter events, 15.5 us)
Async XLA Ops:
  0.6 1.6 copy-start
  0.6 5.0 %copy-start.3 = (bf16[3840,512]{1,0:T(8,128)(2,1)S(1)}, bf16[3840,512]{1,0:T(8,128)(2,1)}, u32[]{:S(2)}) copy-start(bf16[3840,512]{1,0:T(8,128)(2,1)} %param.9) | copy-start | bytes 11796484
  6.8 23.2 %copy-start.8 = (s32[8,8]{1,0:T(8,128)S(1)}, s32[8,8]{1,0:T(8,128)}, u32[]{:S(2)}) copy-start(s32[8,8]{1,0:T(8,128)} %param.13) | copy-start | bytes 772
  6.9 23.2 %copy-start.9 = (s32[8]{0:T(128)S(1)}, s32[8]{0:T(128)}, u32[]{:S(2)}) copy-start(s32[8]{0:T(128)} %param.12) | copy-start | bytes 100
  6.9 23.6 %copy-start.5 = (bf16[256,2048]{1,0:T(8,128)(2,1)S(1)}, bf16[256,2048]{1,0:T(8,128)(2,1)}, u32[]{:S(2)}) copy-start(bf16[256,2048]{1,0:T(8,128)(2,1)} %param.10) | copy-start | bytes 3145732
  8.0 20.3 %all-to-all-start = ((f32[2,512,256]{2,1,0:T(8,128)}), f32[2,512,256]{2,1,0:T(8,128)S(1)}, u32[]{:S(2)}, u32[]{:S(2)}) async-start(f32[2,512,256]{2,1,0:T(8,128)} %bitcast.154), calls=%async_computation | async-start | bytes 2097152 | tf_op jit(solution)/shard_map/all_to_all | solution.py:47
  28.4 6.2 %collective-permute-start = (bf16[256,256]{1,0:T(8,128)(2,1)S(1)}, bf16[256,256]{1,0:T(8,128)(2,1)S(1)}, u32[]{:S(2)}, u32[]{:S(2)}) collective-permute-start(bf16[256,256]{1,0:T(8,128)(2,1)S(1)} %get-tuple-element.6), channel_id=1, source_target_pairs={{0,1},{1,2},{2,3},{3,0},{4,5},{5,6},{6,7},{7,4},{8,9},{9,10},{10,1... | collective-permute-start | bytes 393224 | tf_op jit(solution)/shard_map/ppermute | solution.py:26
  31.1 5.0 %collective-permute-start.1 = (bf16[256,256]{1,0:T(8,128)(2,1)S(1)}, bf16[256,256]{1,0:T(8,128)(2,1)S(1)}, u32[]{:S(2)}, u32[]{:S(2)}) collective-permute-start(bf16[256,256]{1,0:T(8,128)(2,1)S(1)} %get-tuple-element.6), channel_id=1, source_target_pairs={{0,3},{1,0},{2,1},{3,2},{4,7},{5,4},{6,5},{7,6},{8,11},{9,8},{10,9... | collective-permute-start | bytes 393224 | tf_op jit(solution)/shard_map/ppermute | solution.py:32
  34.8 6.2 %collective-permute-start.2 = (bf16[256,256]{1,0:T(8,128)(2,1)S(1)}, bf16[256,256]{1,0:T(8,128)(2,1)S(1)}, u32[]{:S(2)}, u32[]{:S(2)}) collective-permute-start(bf16[256,256]{1,0:T(8,128)(2,1)S(1)} %collective-permute-done), channel_id=1, source_target_pairs={{0,1},{1,2},{2,3},{3,0},{4,5},{5,6},{6,7},{7,4},{8,9},{9,10},{10,1... | collective-permute-start | bytes 393224 | tf_op jit(solution)/shard_map/ppermute | solution.py:26
  49.2 18.3 %all-to-all-start.1 = ((f32[16,2,8,256]{3,2,1,0:T(8,128)}), f32[16,2,8,256]{3,2,1,0:T(8,128)S(1)}, u32[]{:S(2)}, u32[]{:S(2)}) async-start(f32[16,2,8,256]{3,2,1,0:T(8,128)} %broadcast_in_dim.40), calls=%async_computation.1 | async-start | bytes 524288 | tf_op jit(solution)/shard_map/all_to_all | solution.py:62
  76.3 19.1 %all-to-all-start.3 = ((f32[16,256,16]{1,2,0:T(8,128)}), f32[16,256,16]{1,2,0:T(8,128)S(1)}, u32[]{:S(2)}, u32[]{:S(2)}) async-start(f32[16,256,16]{1,2,0:T(8,128)} %broadcast_in_dim.41), calls=%async_computation.3 | async-start | bytes 524288 | tf_op jit(solution)/shard_map/all_to_all | solution.py:62
  92.2 9.0 %copy-start.2 = (bf16[256,2048]{1,0:T(8,128)(2,1)S(1)}, bf16[256,2048]{1,0:T(8,128)(2,1)}, u32[]{:S(2)}) copy-start(bf16[256,2048]{1,0:T(8,128)(2,1)} %param.11) | copy-start | bytes 3145732
  95.4 33.9 %all-to-all-start.2 = ((f32[16,16,16,128]{3,2,1,0:T(8,128)}), f32[16,16,16,128]{3,2,1,0:T(8,128)}, u32[]{:S(2)}, u32[]{:S(2)}) async-start(f32[16,16,16,128]{3,2,1,0:T(8,128)} %bitcast.158), calls=%async_computation.2 | async-start | bytes 4194304 | tf_op jit(solution)/shard_map/all_to_all | solution.py:47
  132.2 21.2 %all-to-all-start.4 = ((bf16[16,16,2048]{2,1,0:T(8,128)(2,1)}), bf16[16,16,2048]{2,1,0:T(8,128)(2,1)S(1)}, u32[]{:S(2)}, u32[]{:S(2)}) async-start(bf16[16,16,2048]{2,1,0:T(8,128)(2,1)} %broadcast_in_dim.42), calls=%async_computation.4 | async-start | bytes 2097152 | tf_op jit(solution)/shard_map/all_to_all | solution.py:62
  137.0 5.9 %copy-start.6 = (bf16[256,2048]{0,1:T(8,128)(2,1)S(1)}, bf16[256,2048]{0,1:T(8,128)(2,1)}, u32[]{:S(2)}) copy-start(bf16[256,2048]{0,1:T(8,128)(2,1)} %copy.97) | copy-start | bytes 3145732
  167.0 7.6 %copy-start.7 = (f32[1024,128]{0,1:T(8,128)S(1)}, f32[1024,128]{0,1:T(8,128)}, u32[]{:S(2)}) copy-start(f32[1024,128]{0,1:T(8,128)} %fusion.33) | copy-start | bytes 1572868
  177.7 31.1 %all-to-all-start.5 = ((f32[4,256,512]{1,2,0:T(8,128)}), f32[4,256,512]{1,2,0:T(8,128)}, u32[]{:S(2)}, u32[]{:S(2)}) async-start(f32[4,256,512]{1,2,0:T(8,128)} %bitcast.159), calls=%async_computation.5 | async-start | bytes 4194304 | tf_op jit(solution)/shard_map/all_to_all | solution.py:47
  220.0 3.5 %copy-start.4 = (bf16[3840,512]{1,0:T(8,128)(2,1)S(1)}, bf16[3840,512]{1,0:T(8,128)(2,1)}, u32[]{:S(2)}) copy-start(bf16[3840,512]{1,0:T(8,128)(2,1)} %param.9) | copy-start | bytes 11796484
  220.0 7.0 %copy-start.1 = (bf16[256,3840]{1,0:T(8,128)(2,1)S(1)}, bf16[256,3840]{1,0:T(8,128)(2,1)}, u32[]{:S(2)}) copy-start(bf16[256,3840]{1,0:T(8,128)(2,1)} %param.7) | copy-start | bytes 5898244
